TPU v7x, 32 devices: a whole 2x2x4 slice. The times are simulated.
32 devices in a mesh: gossip: 4 (over z), fsdp: 2 (over y), tensor: 4 (over x, core).
Axes of the slice: x: 2, y: 2, z: 4, core: 2. Of those that a mesh axis runs over, the one named last changes fastest.
Arguments:
- hidden: bfloat16 [4, 4, 256, 4096], P('gossip', 'fsdp', None, 'tensor'), may hold values from -6 to 6
- cotangent: bfloat16 [4, 4, 256, 4096], P('gossip', 'fsdp', None, 'tensor'), may hold values from -6 to 6
- documents: int32 [4, 4, 256], P('gossip', 'fsdp'), may hold values from 0 to 7, never falling along the last dimension, each value on 1 to 128 neighbouring positions
- q_weight: float32 [4, 4096, 2048], P('gossip', 'fsdp', 'tensor'), may hold values from -0.09375 to 0.09375
- k_weight: float32 [4, 4096, 512], P('gossip', 'fsdp', 'tensor'), may hold values from -0.09375 to 0.09375
- v_weight: float32 [4, 4096, 512], P('gossip', 'fsdp', 'tensor'), may hold values from -0.09375 to 0.09375
- o_weight: float32 [4, 4096, 2048], P('gossip', 'fsdp', 'tensor'), may hold values from -0.125 to 0.125
- edge_weight: float32 [4], P('gossip'), may hold values from 0.1 to 0.45
Outputs:
- new_q_weight: float32 [4, 4096, 2048], P('gossip', 'fsdp', 'tensor')
- new_k_weight: float32 [4, 4096, 512], P('gossip', 'fsdp', 'tensor')
- new_v_weight: float32 [4, 4096, 512], P('gossip', 'fsdp', 'tensor')
- new_o_weight: float32 [4, 4096, 2048], P('gossip', 'fsdp', 'tensor')
Inputs may be any that keep to these rules, and one draw needn't show every extreme that they name: `documents`: document ids never fall along a sequence; each document spans 1 to 128 positions, and some document spans exactly 128.
All inputs are finite; a program needn't handle non-finite values.
Results may differ from a plain program's by a relative error of at most 0.007.
Values may be sent and summed in bfloat16 or wider, within the bound.
No kernel may reach another device: no remote copies, remote signals or barrier semaphores. Data moves between devices by JAX's collectives and lax.ppermute only.
A program may use at most 128 MiB of HBM per device.

v0:
```python
import math
import jax
import jax.numpy as jnp
from jax import lax
from jax.sharding import PartitionSpec as P

HD = 128
rope_theta = 500000.0
learn_rate = 0.001
norm_eps = 1e-05


def passed_along(shard, axis, by):
    count = lax.axis_size(axis)
    return lax.ppermute(shard, axis, [(i, (i + by) % count) for i in range(count)])


def contract(form, left, right):
    return jnp.einsum(form, left, right, preferred_element_type=jnp.float32)


def rope_tables(length, head_size):
    half_dim = head_size // 2
    positions = jnp.arange(length, dtype=jnp.float32)
    freqs = jnp.exp(
        jnp.arange(half_dim, dtype=jnp.float32) * (-2.0 / head_size * math.log(rope_theta))
    )
    angles = positions[:, None] * freqs[None, :]
    return (jnp.cos(angles), jnp.sin(angles))


def rotate(values, cosine, sine_table):
    half_dim = values.shape[-1] // 2
    first_half = values[..., :half_dim]
    second_half = values[..., half_dim:]
    return jnp.concatenate(
        [
            first_half * cosine - second_half * sine_table,
            second_half * cosine + first_half * sine_table,
        ],
        -1,
    )


def unrotate(values, cosine, sine_table):
    half_dim = values.shape[-1] // 2
    first_half = values[..., :half_dim]
    second_half = values[..., half_dim:]
    return jnp.concatenate(
        [
            first_half * cosine + second_half * sine_table,
            second_half * cosine - first_half * sine_table,
        ],
        -1,
    )


def attention_grads(proj, d_ctx, documents, heads_q, heads_k):
    seq_count, length = documents.shape
    group_size = heads_q // heads_k
    q_cols = heads_q * HD
    kv_cols = heads_k * HD
    cosine, sine_table = rope_tables(length, HD)
    cos_query = cosine[None, :, None, None, :]
    sin_query = sine_table[None, :, None, None, :]
    cos_key = cosine[None, :, None, :]
    sin_key = sine_table[None, :, None, :]
    query = rotate(
        proj[..., :q_cols].reshape(seq_count, length, heads_k, group_size, HD), cos_query, sin_query
    ).astype(jnp.bfloat16)
    key_rot = rotate(
        proj[..., q_cols : q_cols + kv_cols].reshape(seq_count, length, heads_k, HD),
        cos_key,
        sin_key,
    ).astype(jnp.bfloat16)
    value_b = (
        proj[..., q_cols + kv_cols :].reshape(seq_count, length, heads_k, HD).astype(jnp.bfloat16)
    )
    d_out = d_ctx.reshape(seq_count, length, heads_k, group_size, HD).astype(jnp.bfloat16)
    score_scale = 1.0 / math.sqrt(HD)
    scores = contract("bqhgd,bkhd->bhgqk", query, key_rot) * score_scale
    positions = jnp.arange(length)
    causal = positions[:, None] >= positions[None, :]
    same_doc = documents[:, :, None] == documents[:, None, :]
    allowed = (causal[None] & same_doc)[:, None, None, :, :]
    exp_scores = jnp.where(allowed, jnp.exp(scores), 0.0)
    probs_f = exp_scores / jnp.sum(exp_scores, -1, keepdims=True)
    probs_b = probs_f.astype(jnp.bfloat16)
    context = contract("bhgqk,bkhd->bqhgd", probs_b, value_b).astype(jnp.bfloat16)
    d_probs = contract("bqhgd,bkhd->bhgqk", d_out, value_b)
    d_value = contract("bhgqk,bqhgd->bkhd", probs_b, d_out).astype(jnp.bfloat16)
    delta_sum = jnp.sum(probs_f * d_probs, -1, keepdims=True)
    d_scores = (probs_f * (d_probs - delta_sum) * score_scale).astype(jnp.bfloat16)
    d_query = contract("bhgqk,bkhd->bqhgd", d_scores, key_rot)
    d_key = contract("bhgqk,bqhgd->bkhd", d_scores, query)
    d_query = unrotate(d_query, cos_query, sin_query).astype(jnp.bfloat16)
    d_key = unrotate(d_key, cos_key, sin_key).astype(jnp.bfloat16)
    d_proj = jnp.concatenate(
        [
            d_query.reshape(seq_count, length, q_cols),
            d_key.reshape(seq_count, length, kv_cols),
            d_value.reshape(seq_count, length, kv_cols),
        ],
        -1,
    )
    return (d_proj, context.reshape(seq_count, length, q_cols))


def mix_three(center, from_low, from_high, c_low, c_high):
    return center + c_low * (from_low - center) + c_high * (from_high - center)


def body(hidden, cotangent, documents, q_weight, k_weight, v_weight, o_weight, edge_weight):
    full_hidden, full_cotan = (
        lax.all_gather(hidden, "tensor", axis=3, tiled=True),
        lax.all_gather(cotangent, "tensor", axis=3, tiled=True),
    )
    seq_count, length, model_width = full_hidden.shape[1:]
    token_rows = seq_count * length
    hidden_f = full_hidden[0].reshape(token_rows, model_width).astype(jnp.float32)
    normed = (
        hidden_f * lax.rsqrt(jnp.mean(hidden_f * hidden_f, -1, keepdims=True) + norm_eps)
    ).astype(jnp.bfloat16)
    cotan_rows = full_cotan[0].reshape(token_rows, model_width)
    q_cols = q_weight.shape[2]
    kv_cols = k_weight.shape[2]
    proj_cols = q_cols + 2 * kv_cols
    packed = jnp.concatenate([q_weight[0], k_weight[0], v_weight[0], o_weight[0]], 1).astype(
        jnp.bfloat16
    )
    block_rows = lax.all_gather(packed, "fsdp", axis=0, tiled=True)
    left = normed
    right = cotan_rows
    proj = jnp.dot(left, block_rows[:, :proj_cols], preferred_element_type=jnp.float32)
    d_ctx = jnp.dot(right, block_rows[:, proj_cols:], preferred_element_type=jnp.float32)
    d_proj, context = attention_grads(
        proj.reshape(seq_count, length, proj_cols),
        d_ctx.reshape(seq_count, length, q_cols),
        documents[0],
        q_cols // HD,
        kv_cols // HD,
    )
    d_proj = d_proj.reshape(token_rows, proj_cols)
    context = context.reshape(token_rows, q_cols)
    contract_rows = (((0,), (0,)), ((), ()))
    left = normed
    right = cotan_rows
    first_part = lax.dot_general(left, d_proj, contract_rows, preferred_element_type=jnp.float32)
    second_part = lax.dot_general(right, context, contract_rows, preferred_element_type=jnp.float32)
    gradients = lax.psum_scatter(
        jnp.concatenate([first_part, second_part], 1).astype(jnp.bfloat16),
        "fsdp",
        scatter_dimension=0,
        tiled=True,
    ).astype(jnp.float32)
    grad_q = gradients[None, :, :q_cols]
    grad_k = gradients[None, :, q_cols : q_cols + kv_cols]
    grad_v = gradients[None, :, q_cols + kv_cols : proj_cols]
    grad_o = gradients[None, :, proj_cols:]
    c_high = edge_weight[0]
    new_q = q_weight - learn_rate * grad_q
    new_k = k_weight - learn_rate * grad_k
    new_v = v_weight - learn_rate * grad_v
    new_o = o_weight - learn_rate * grad_o
    from_low = passed_along((new_q, new_k, new_v, new_o, edge_weight), "gossip", 1)
    from_high = passed_along((new_q, new_k, new_v, new_o), "gossip", -1)
    c_low = from_low[4][0]
    return (
        mix_three(new_q, from_low[0], from_high[0], c_low, c_high),
        mix_three(new_k, from_low[1], from_high[1], c_low, c_high),
        mix_three(new_v, from_low[2], from_high[2], c_low, c_high),
        mix_three(new_o, from_low[3], from_high[3], c_low, c_high),
    )


def solution(mesh):
    return jax.shard_map(
        body,
        mesh=mesh,
        in_specs=(
            P("gossip", "fsdp", None, "tensor"),
            P("gossip", "fsdp", None, "tensor"),
            P("gossip", "fsdp", None),
            P("gossip", "fsdp", "tensor"),
            P("gossip", "fsdp", "tensor"),
            P("gossip", "fsdp", "tensor"),
            P("gossip", "fsdp", "tensor"),
            P("gossip"),
        ),
        out_specs=(
            P("gossip", "fsdp", "tensor"),
            P("gossip", "fsdp", "tensor"),
            P("gossip", "fsdp", "tensor"),
            P("gossip", "fsdp", "tensor"),
        ),
        check_vma=False,
    )
```

profile of v0, /device:TPU:0, one launch (start us, length us, event | category | flops | bytes accessed | tf_op | source)
XLA Modules:
  0.0 878.4 jit_solution(919153522589254380)
XLA Ops:
  9.6 4.0 convert_bitcast_fusion
  17.9 28.8 %all-gather.4.cloned.1.call-done = bf16[1,2,256,4096]{3,2,1,0:T(8,128)(2,1)} async-done(((bf16[1,2,256,1024]{3,2,1,0:T(8,128)(2,1)}), bf16[1,2,256,4096]{3,2,1,0:T(8,128)(2,1)}) %all-gather.4.cloned.1.call-update) | async-done | bytes 4194320 | tf_op jit(solution)/shard_map/all_gather | solution.py:115
  50.2 3.4 fusion.1
  53.6 124.3 %all-gather.6.cloned.1.call-done = bf16[4096,1280]{1,0:T(8,128)(2,1)} async-done(((bf16[2048,1280]{1,0:T(8,128)(2,1)}), bf16[4096,1280]{1,0:T(8,128)(2,1)}) %all-gather.6.cloned.1.call-update) | async-done | bytes 10485776 | tf_op jit(solution)/shard_map/all_gather | solution.py:131
  177.9 7.3 fusion.2
  189.2 24.8 %all-gather.8.cloned.1.call-done = bf16[1,2,256,4096]{3,2,1,0:T(8,128)(2,1)} async-done(((bf16[1,2,256,1024]{3,2,1,0:T(8,128)(2,1)}), bf16[1,2,256,4096]{3,2,1,0:T(8,128)(2,1)}) %all-gather.8.cloned.1.call-update) | async-done | bytes 4194320 | tf_op jit(solution)/shard_map/all_gather | solution.py:116
  214.0 6.7 fusion.23
  230.9 5.0 fusion.3
  235.9 4.3 convolution_convert_fusion
  240.2 9.6 %pad_maximum_fusion = bf16[4096,1280]{0,1:T(8,128)(2,1)} fusion(bf16[4096,512]{0,1:T(8,128)(2,1)S(1)} %fusion.3, bf16[4096,768]{0,1:T(8,128)(2,1)S(1)} %convolution_convert_fusion), kind=kLoop, calls=%fused_computation | loop fusion | flops 20971520 | bytes 20971520 | tf_op jit(solution)/shard_map/concatenate | solution.py:151
  249.8 5.3 copy.49
  255.2 6.0 copy.52
  263.8 108.0 %reduce-scatter.2.cloned.1.call-done = bf16[2048,1280]{0,1:T(8,128)(2,1)} async-done(((bf16[4096,1280]{0,1:T(8,128)(2,1)}), bf16[2048,1280]{0,1:T(8,128)(2,1)}) %reduce-scatter.2.cloned.1.call-update) | async-done | bytes 5242896 | tf_op jit(solution)/shard_map/reduce_scatter | solution.py:150
  371.8 4.0 convert_element_type.107
  375.9 4.0 copy-done
  382.1 10.4 %fusion.6 = (f32[1,2048,512]{1,2,0:T(8,128)}, f32[1,2048,512]{1,2,0:T(8,128)}) fusion(f32[1,2048,512]{1,2,0:T(8,128)} %copy.52, f32[2048,1280]{0,1:T(8,128)} %copy-done, f32[1,2048,512]{1,2,0:T(8,128)S(1)} %copy-done.2), kind=kLoop, calls=%fused_computation.14 | loop fusion | flops 4194304 | bytes 25165824 | tf_op jit(solution)/shard_map/sub | solution.py:164
  398.3 210.9 %collective-permute-done = f32[1]{0:T(128)} collective-permute-done((f32[1]{0:T(128)}, f32[1]{0:T(128)}, u32[]{:S(2)}, u32[]{:S(2)}) %collective-permute-start) | collective-permute-done | bytes 36 | tf_op jit(solution)/shard_map/ppermute | solution.py:15
  609.3 3.8 collective-permute-start.2
  613.1 202.5 %collective-permute-done.3 = f32[1,2048,128]{1,2,0:T(8,128)S(1)} collective-permute-done((f32[1,2048,128]{1,2,0:T(8,128)S(1)}, f32[1,2048,128]{1,2,0:T(8,128)S(1)}, u32[]{:S(2)}, u32[]{:S(2)}) %collective-permute-start.3) | collective-permute-done | bytes 1048608 | tf_op jit(solution)/shard_map/ppermute | solution.py:15
  820.7 18.3 %collective-permute-done.4 = f32[1,2048,128]{1,2,0:T(8,128)} collective-permute-done((f32[1,2048,128]{1,2,0:T(8,128)S(1)}, f32[1,2048,128]{1,2,0:T(8,128)}, u32[]{:S(2)}, u32[]{:S(2)}) %collective-permute-start.4) | collective-permute-done | bytes 1048608 | tf_op jit(solution)/shard_map/ppermute | solution.py:15
  842.8 9.2 %multiply_add_fusion = f32[1,2048,512]{1,2,0:T(8,128)} fusion(f32[1,2048,512]{1,2,0:T(8,128)} %collective-permute-done.8, f32[1,2048,512]{1,2,0:T(8,128)} %get-tuple-element.12, f32[1,2048,512]{1,2,0:T(8,128)} %collective-permute-done.7, f32[]{:T(128)} %bitcast.169, f32[]{:T(128)} %bitcast.46), kind=kLoop, calls=%fused_computation.21 | loop fusion | flops 6291456 | bytes 16777224 | tf_op jit(solution)/shard_map/add | solution.py:110
  852.0 5.3 copy.56
  857.3 9.2 %multiply_add_fusion.1 = f32[1,2048,512]{1,2,0:T(8,128)} fusion(f32[1,2048,512]{1,2,0:T(8,128)} %collective-permute-done.2, f32[1,2048,512]{1,2,0:T(8,128)} %get-tuple-element.13, f32[1,2048,512]{1,2,0:T(8,128)} %collective-permute-done.1, f32[]{:T(128)} %bitcast.167, f32[]{:T(128)} %bitcast.46), kind=kLoop, calls=%fused_computation.22 | loop fusion | flops 6291456 | bytes 16777224 | tf_op jit(solution)/shard_map/add | solution.py:110
  866.6 5.3 copy.53
  (82 shorter events, 43.1 us)
Async XLA Ops:
  7.2 39.6 %all-gather.4.cloned.1.call-start = ((), (), s32[]{:S(2)}) async-start(), calls=%async_computation.1 | async-start | bytes 5242880 | tf_op jit(solution)/shard_map/all_gather | solution.py:115
  7.9 170.0 %all-gather.6.cloned.1.call-start = ((), (), s32[]{:S(2)}) async-start(), calls=%async_computation.2 | async-start | bytes 15728640 | tf_op jit(solution)/shard_map/all_gather | solution.py:131
  16.4 197.5 %all-gather.8.cloned.1.call-start = ((), (), s32[]{:S(2)}) async-start(), calls=%async_computation.3 | async-start | bytes 5242880 | tf_op jit(solution)/shard_map/all_gather | solution.py:116
  17.2 354.7 %reduce-scatter.2.cloned.1.call-start = ((), (), s32[]{:S(2)}) async-start(), calls=%async_computation.4 | async-start | bytes 15728640 | tf_op jit(solution)/shard_map/reduce_scatter | solution.py:150
  46.8 3.4 copy-start.1
  185.2 1.1 copy-start.9
  214.0 7.9 copy-start.8
  230.9 5.0 copy-start.3
  255.2 6.0 copy-start.4
  255.2 7.3 copy-start.5
  371.8 8.1 copy-start.6
  371.8 8.1 copy-start.7
  375.9 4.0 copy-start
  379.9 2.2 copy-start.2
  380.3 229.0 %collective-permute-start.5 = (f32[1,2048,128]{1,2,0:T(8,128)S(1)}, f32[1,2048,128]{1,2,0:T(8,128)}, u32[]{:S(2)}, u32[]{:S(2)}) collective-permute-start(f32[1,2048,128]{1,2,0:T(8,128)S(1)} %get-tuple-element.14), channel_id=1, source_target_pairs={{0,8},{8,16},{16,24},{24,0},{1,9},{9,17},{17,25},{25,1},{2,10},{10... | collective-permute-start | bytes 3145736 | tf_op jit(solution)/shard_map/ppermute | solution.py:15
  392.5 450.3 %collective-permute-start.7 = (f32[1,2048,512]{1,2,0:T(8,128)}, f32[1,2048,512]{1,2,0:T(8,128)}, u32[]{:S(2)}, u32[]{:S(2)}) collective-permute-start(f32[1,2048,512]{1,2,0:T(8,128)} %get-tuple-element.12), channel_id=1, source_target_pairs={{0,8},{8,16},{16,24},{24,0},{1,9},{9,17},{17,25},{25,1},{2,10},{10... | collective-permute-start | bytes 12582920 | tf_op jit(solution)/shard_map/ppermute | solution.py:15
  394.0 448.8 %collective-permute-start.8 = (f32[1,2048,512]{1,2,0:T(8,128)}, f32[1,2048,512]{1,2,0:T(8,128)}, u32[]{:S(2)}, u32[]{:S(2)}) collective-permute-start(f32[1,2048,512]{1,2,0:T(8,128)} %get-tuple-element.12), channel_id=1, source_target_pairs={{0,24},{8,0},{16,8},{24,16},{1,25},{9,1},{17,9},{25,17},{2,26},{10... | collective-permute-start | bytes 12582920 | tf_op jit(solution)/shard_map/ppermute | solution.py:15
  396.3 216.8 %collective-permute-start.6 = (f32[1,2048,128]{1,2,0:T(8,128)S(1)}, f32[1,2048,128]{1,2,0:T(8,128)S(1)}, u32[]{:S(2)}, u32[]{:S(2)}) collective-permute-start(f32[1,2048,128]{1,2,0:T(8,128)S(1)} %get-tuple-element.14), channel_id=1, source_target_pairs={{0,24},{8,0},{16,8},{24,16},{1,25},{9,1},{17,9},{25,17},{2,26},{10... | collective-permute-start | bytes 3145736 | tf_op jit(solution)/shard_map/ppermute | solution.py:15
  397.8 211.4 %collective-permute-start = (f32[1]{0:T(128)}, f32[1]{0:T(128)}, u32[]{:S(2)}, u32[]{:S(2)}) collective-permute-start(f32[1]{0:T(128)} %param.15), channel_id=1, source_target_pairs={{0,8},{8,16},{16,24},{24,0},{1,9},{9,17},{17,25},{25,1},{2,10},{10... | collective-permute-start | bytes 20 | tf_op jit(solution)/shard_map/ppermute | solution.py:15
  609.3 248.1 %collective-permute-start.1 = (f32[1,2048,512]{1,2,0:T(8,128)}, f32[1,2048,512]{1,2,0:T(8,128)}, u32[]{:S(2)}, u32[]{:S(2)}) collective-permute-start(f32[1,2048,512]{1,2,0:T(8,128)} %get-tuple-element.13), channel_id=1, source_target_pairs={{0,8},{8,16},{16,24},{24,0},{1,9},{9,17},{17,25},{25,1},{2,10},{10... | collective-permute-start | bytes 12582920 | tf_op jit(solution)/shard_map/ppermute | solution.py:15
  609.3 248.1 %collective-permute-start.2 = (f32[1,2048,512]{1,2,0:T(8,128)}, f32[1,2048,512]{1,2,0:T(8,128)}, u32[]{:S(2)}, u32[]{:S(2)}) collective-permute-start(f32[1,2048,512]{1,2,0:T(8,128)} %get-tuple-element.13), channel_id=1, source_target_pairs={{0,24},{8,0},{16,8},{24,16},{1,25},{9,1},{17,9},{25,17},{2,26},{10... | collective-permute-start | bytes 12582920 | tf_op jit(solution)/shard_map/ppermute | solution.py:15
  613.1 202.5 %collective-permute-start.3 = (f32[1,2048,128]{1,2,0:T(8,128)S(1)}, f32[1,2048,128]{1,2,0:T(8,128)S(1)}, u32[]{:S(2)}, u32[]{:S(2)}) collective-permute-start(f32[1,2048,128]{1,2,0:T(8,128)S(1)} %get-tuple-element.15), channel_id=1, source_target_pairs={{0,8},{8,16},{16,24},{24,0},{1,9},{9,17},{17,25},{25,1},{2,10},{10... | collective-permute-start | bytes 3145736 | tf_op jit(solution)/shard_map/ppermute | solution.py:15
  815.6 1.0 copy-start.10
  816.6 22.5 %collective-permute-start.4 = (f32[1,2048,128]{1,2,0:T(8,128)S(1)}, f32[1,2048,128]{1,2,0:T(8,128)}, u32[]{:S(2)}, u32[]{:S(2)}) collective-permute-start(f32[1,2048,128]{1,2,0:T(8,128)S(1)} %get-tuple-element.15), channel_id=1, source_target_pairs={{0,24},{8,0},{16,8},{24,16},{1,25},{9,1},{17,9},{25,17},{2,26},{10... | collective-permute-start | bytes 3145736 | tf_op jit(solution)/shard_map/ppermute | solution.py:15
  (1 other events, 0.9 us)
Sparse Core Ops, SparseCore 0:
  9.6 37.1 all-gather.3
  48.3 129.5 all-gather.5
  179.4 34.4 all-gather.7
  249.9 121.8 reduce-scatter.1
where the time goes:
time: 879 us; the launch traced here: 878 us
  waiting for transfers between devices  719 us (82%)
  other arithmetic  65.3 us (7%)
  local copies, waits for them, and re-layouts  38.7 us (4%)
  matrix products  29.3 us (3%)
  between operations  14.7 us (2%)
  starting transfers between devices  11.4 us (1%)
    ppermute x9, waiting for transfers between devices, passed_along(): lax.ppermute(shard, axis, [(i, (i + by) % count) for i in range(count)])  432 us
    all_gather x1, waiting for transfers between devices, body(): block_rows = lax.all_gather(packed, 'fsdp', axis=0, tiled=True)  124 us
    reduce_scatter x1, waiting for transfers between devices, body(): lax.psum_scatter(jnp.concatenate([first_part, second_part], 1).astype(jnp...  108 us
    unnamed x34, local copies, waits for them, and re-layouts  33.9 us
    all_gather x1, waiting for transfers between devices, body(): lax.all_gather(hidden, 'tensor', axis=3, tiled=True)  28.8 us
    all_gather x1, waiting for transfers between devices, body(): lax.all_gather(cotangent, 'tensor', axis=3, tiled=True)  24.8 us
    add x4, other arithmetic, mix_three(): return center + c_low * (from_low - center) + c_high * (from_high - center)  23 us
  transfers between devices with their start and end apart: 13, of which 7 were waited for; matrix products, arithmetic and copies ran while one was open for 8% of the time, Pallas kernels for 0%

commit v1 on v0

--- a/solution.py
+++ b/solution.py
@@ -8,6 +8,18 @@
 rope_theta = 500000.0
 learn_rate = 0.001
 norm_eps = 1e-05
+
+
+def collect(x, axis, dim):
+    ways, here, turn = (lax.axis_size(axis), lax.axis_index(axis), x.shape[dim])
+    line, have = (x, 1)
+    while have < ways:
+        line = jnp.concatenate(
+            [line, lax.ppermute(line, axis, [(d, (d - have) % ways) for d in range(ways)])],
+            axis=dim,
+        )
+        have = 2 * have
+    return jnp.roll(line, here * turn, axis=dim)
 
 
 def passed_along(shard, axis, by):
@@ -113,7 +125,7 @@
 def body(hidden, cotangent, documents, q_weight, k_weight, v_weight, o_weight, edge_weight):
     full_hidden, full_cotan = (
         lax.all_gather(hidden, "tensor", axis=3, tiled=True),
-        lax.all_gather(cotangent, "tensor", axis=3, tiled=True),
+        collect(cotangent, "tensor", 3),
     )
     seq_count, length, model_width = full_hidden.shape[1:]
     token_rows = seq_count * length

time: 879 us -> 873 us (level)
  waiting for transfers between devices: 719 us -> 693 us
  local copies, waits for them, and re-layouts: 38.7 us -> 55.4 us
    ppermute x0 -> x2, waiting for transfers between devices: none -> 81.7 us  [collect(): lax.ppermute(line, axis, [(d, (d - have) % ways) for d in range(ways)])]
    all_gather x1, waiting for transfers between devices: 124 us -> 71.7 us  [body(): block_rows = lax.all_gather(packed, 'fsdp', axis=0, tiled=True)]
    all_gather x1, waiting for transfers between devices: 28.8 us -> 0.01 us  [body(): lax.all_gather(hidden, 'tensor', axis=3, tiled=True)]
    all_gather x1 -> x0, waiting for transfers between devices: 24.8 us -> none  [body(): lax.all_gather(cotangent, 'tensor', axis=3, tiled=True)]
    dot_general x0 -> x2, local copies, waits for them, and re-layouts: none -> 10.9 us  [body(): jnp.dot(right, block_rows[:, proj_cols:], preferred_element_type=jnp.floa...]
    unnamed x34 -> x41, local copies, waits for them, and re-layouts: 33.9 us -> 38.5 us
  transfers between devices with their start and end apart: 13 -> 14, of which waited for: 7 -> 7; matrix products, arithmetic and copies ran while one was open for 8% -> 8% of each run, Pallas kernels for 0% -> 0%
where the time goes in v1:
time: 873 us; the launch traced here: 872 us
  waiting for transfers between devices  693 us (79%)
  other arithmetic  66.8 us (8%)
  local copies, waits for them, and re-layouts  55.4 us (6%)
  matrix products  27 us (3%)
  starting transfers between devices  15.4 us (2%)
  between operations  14.7 us (2%)
    ppermute x9, waiting for transfers between devices, passed_along(): lax.ppermute(shard, axis, [(i, (i + by) % count) for i in range(count)])  430 us
    reduce_scatter x1, waiting for transfers between devices, body(): lax.psum_scatter(jnp.concatenate([first_part, second_part], 1).astype(jnp...  108 us
    ppermute x2, waiting for transfers between devices, collect(): lax.ppermute(line, axis, [(d, (d - have) % ways) for d in range(ways)])  81.7 us
    all_gather x1, waiting for transfers between devices, body(): block_rows = lax.all_gather(packed, 'fsdp', axis=0, tiled=True)  71.7 us
    unnamed x41, local copies, waits for them, and re-layouts  38.5 us
    add x4, other arithmetic, mix_three(): return center + c_low * (from_low - center) + c_high * (from_high - center)  23 us
  transfers between devices with their start and end apart: 14, of which 7 were waited for; matrix products, arithmetic and copies ran while one was open for 8% of the time, Pallas kernels for 0%

profile of v1, /device:TPU:0, one launch (start us, length us, event | category | flops | bytes accessed | tf_op | source)
XLA Modules:
  0.0 872.0 jit_solution(9807207163967400576)
XLA Ops:
  9.6 4.0 convert_bitcast_fusion
  20.1 34.1 %collective-permute-done = bf16[1,2,256,1024]{3,2,1,0:T(8,128)(2,1)S(1)} collective-permute-done((bf16[1,2,256,1024]{3,2,1,0:T(8,128)(2,1)S(1)}, bf16[1,2,256,1024]{3,2,1,0:T(8,128)(2,1)S(1)}, u32[]{:S(2)}, u32[]{:S(2)}) %collective-permute-start) | collective-permute-done | bytes 1048608 | tf_op jit(solution)/shard_map/ppermute | solution.py:18
  56.9 47.6 %collective-permute-done.1 = bf16[1,2,256,2048]{3,2,1,0:T(8,128)(2,1)} collective-permute-done((bf16[1,2,256,2048]{3,2,1,0:T(8,128)(2,1)}, bf16[1,2,256,2048]{3,2,1,0:T(8,128)(2,1)}, u32[]{:S(2)}, u32[]{:S(2)}) %collective-permute-start.1) | collective-permute-done | bytes 2097184 | tf_op jit(solution)/shard_map/ppermute | solution.py:18
  117.3 71.7 %all-gather.5.cloned.1.call-done = bf16[4096,1280]{1,0:T(8,128)(2,1)} async-done(((bf16[2048,1280]{1,0:T(8,128)(2,1)}), bf16[4096,1280]{1,0:T(8,128)(2,1)}) %all-gather.5.cloned.1.call-update) | async-done | bytes 10485776 | tf_op jit(solution)/shard_map/all_gather | solution.py:143
  189.0 7.1 fusion.2
  197.4 4.5 slice_bitcast_fusion.2
  201.9 6.4 copy.73
  210.8 4.5 fusion.18
  224.5 4.7 convolution_convert_fusion.1
  229.2 4.5 convolution_convert_fusion
  233.7 9.6 %pad_maximum_fusion = bf16[4096,1280]{0,1:T(8,128)(2,1)} fusion(bf16[4096,512]{0,1:T(8,128)(2,1)S(1)} %convolution_convert_fusion.1, bf16[4096,768]{0,1:T(8,128)(2,1)S(1)} %convolution_convert_fusion), kind=kLoop, calls=%fused_computation | loop fusion | flops 20971520 | bytes 20971520 | tf_op jit(solution)/shard_map/concatenate | solution.py:163
  243.4 5.3 copy.49
  248.7 6.0 copy.52
  257.4 108.0 %reduce-scatter.2.cloned.1.call-done = bf16[2048,1280]{0,1:T(8,128)(2,1)} async-done(((bf16[4096,1280]{0,1:T(8,128)(2,1)}), bf16[2048,1280]{0,1:T(8,128)(2,1)}) %reduce-scatter.2.cloned.1.call-update) | async-done | bytes 5242896 | tf_op jit(solution)/shard_map/reduce_scatter | solution.py:162
  365.4 4.0 convert_element_type.96
  369.5 4.0 copy-done
  375.7 10.4 %fusion.5 = (f32[1,2048,512]{1,2,0:T(8,128)}, f32[1,2048,512]{1,2,0:T(8,128)}) fusion(f32[1,2048,512]{1,2,0:T(8,128)} %copy.52, f32[2048,1280]{0,1:T(8,128)} %copy-done, f32[1,2048,512]{1,2,0:T(8,128)S(1)} %copy-done.2), kind=kLoop, calls=%fused_computation.13 | loop fusion | flops 4194304 | bytes 25165824 | tf_op jit(solution)/shard_map/sub | solution.py:176
  393.2 209.7 %collective-permute-done.2 = f32[1]{0:T(128)} collective-permute-done((f32[1]{0:T(128)}, f32[1]{0:T(128)}, u32[]{:S(2)}, u32[]{:S(2)}) %collective-permute-start.2) | collective-permute-done | bytes 36 | tf_op jit(solution)/shard_map/ppermute | solution.py:27
  606.7 202.5 %collective-permute-done.5 = f32[1,2048,128]{1,2,0:T(8,128)S(1)} collective-permute-done((f32[1,2048,128]{1,2,0:T(8,128)S(1)}, f32[1,2048,128]{1,2,0:T(8,128)S(1)}, u32[]{:S(2)}, u32[]{:S(2)}) %collective-permute-start.5) | collective-permute-done | bytes 1048608 | tf_op jit(solution)/shard_map/ppermute | solution.py:27
  814.3 18.3 %collective-permute-done.6 = f32[1,2048,128]{1,2,0:T(8,128)} collective-permute-done((f32[1,2048,128]{1,2,0:T(8,128)S(1)}, f32[1,2048,128]{1,2,0:T(8,128)}, u32[]{:S(2)}, u32[]{:S(2)}) %collective-permute-start.6) | collective-permute-done | bytes 1048608 | tf_op jit(solution)/shard_map/ppermute | solution.py:27
  836.4 9.2 %multiply_add_fusion = f32[1,2048,512]{1,2,0:T(8,128)} fusion(f32[1,2048,512]{1,2,0:T(8,128)} %collective-permute-done.10, f32[1,2048,512]{1,2,0:T(8,128)} %get-tuple-element.12, f32[1,2048,512]{1,2,0:T(8,128)} %collective-permute-done.9, f32[]{:T(128)} %bitcast.178, f32[]{:T(128)} %bitcast.50), kind=kLoop, calls=%fused_computation.21 | loop fusion | flops 6291456 | bytes 16777224 | tf_op jit(solution)/shard_map/add | solution.py:122
  845.6 5.3 copy.56
  850.9 9.2 %multiply_add_fusion.1 = f32[1,2048,512]{1,2,0:T(8,128)} fusion(f32[1,2048,512]{1,2,0:T(8,128)} %collective-permute-done.4, f32[1,2048,512]{1,2,0:T(8,128)} %get-tuple-element.13, f32[1,2048,512]{1,2,0:T(8,128)} %collective-permute-done.3, f32[]{:T(128)} %bitcast.176, f32[]{:T(128)} %bitcast.50), kind=kLoop, calls=%fused_computation.22 | loop fusion | flops 6291456 | bytes 16777224 | tf_op jit(solution)/shard_map/add | solution.py:122
  860.2 5.3 copy.53
  (94 shorter events, 61.0 us)
Async XLA Ops:
  7.2 103.3 %all-gather.3.cloned.1.call-start = ((), (), s32[]{:S(2)}) async-start(), calls=%async_computation.1 | async-start | bytes 5242880 | tf_op jit(solution)/shard_map/all_gather | solution.py:127
  7.9 181.1 %all-gather.5.cloned.1.call-start = ((), (), s32[]{:S(2)}) async-start(), calls=%async_computation.2 | async-start | bytes 15728640 | tf_op jit(solution)/shard_map/all_gather | solution.py:143
  16.4 39.8 %copy-start.12 = (s32[1,2,256]{2,1,0:T(2,128)S(1)}, s32[1,2,256]{2,1,0:T(2,128)}, u32[]{:S(2)}) copy-start(s32[1,2,256]{2,1,0:T(2,128)} %param.10) | copy-start | bytes 6148
  16.4 349.0 %reduce-scatter.2.cloned.1.call-start = ((), (), s32[]{:S(2)}) async-start(), calls=%async_computation.3 | async-start | bytes 15728640 | tf_op jit(solution)/shard_map/reduce_scatter | solution.py:162
  17.6 36.6 %collective-permute-start = (bf16[1,2,256,1024]{3,2,1,0:T(8,128)(2,1)S(1)}, bf16[1,2,256,1024]{3,2,1,0:T(8,128)(2,1)S(1)}, u32[]{:S(2)}, u32[]{:S(2)}) collective-permute-start(bf16[1,2,256,1024]{3,2,1,0:T(8,128)(2,1)S(1)} %copy-done.3), channel_id=1, source_target_pairs={{0,3},{1,0},{2,1},{3,2},{4,7},{5,4},{6,5},{7,6},{8,11},{9,8},{10,9... | collective-permute-start | bytes 3145736 | tf_op jit(solution)/shard_map/ppermute | solution.py:18
  55.7 48.8 %collective-permute-start.1 = (bf16[1,2,256,2048]{3,2,1,0:T(8,128)(2,1)}, bf16[1,2,256,2048]{3,2,1,0:T(8,128)(2,1)}, u32[]{:S(2)}, u32[]{:S(2)}) collective-permute-start(bf16[1,2,256,2048]{3,2,1,0:T(8,128)(2,1)} %pad_maximum_fusion.2), channel_id=1, source_target_pairs={{0,2},{1,3},{2,0},{3,1},{4,6},{5,7},{6,4},{7,5},{8,10},{9,11},{10,... | collective-permute-start | bytes 6291464 | tf_op jit(solution)/shard_map/ppermute | solution.py:18
  110.4 3.4 copy-start.1
  208.6 2.2 copy-start.7
  224.5 4.7 copy-start.4
  248.7 6.0 copy-start.5
  248.7 7.3 copy-start.6
  365.4 8.1 copy-start.8
  365.4 8.1 copy-start.9
  369.4 4.0 copy-start
  373.5 2.2 copy-start.2
  373.9 229.0 %collective-permute-start.7 = (f32[1,2048,128]{1,2,0:T(8,128)S(1)}, f32[1,2048,128]{1,2,0:T(8,128)}, u32[]{:S(2)}, u32[]{:S(2)}) collective-permute-start(f32[1,2048,128]{1,2,0:T(8,128)S(1)} %get-tuple-element.14), channel_id=1, source_target_pairs={{0,8},{8,16},{16,24},{24,0},{1,9},{9,17},{17,25},{25,1},{2,10},{10... | collective-permute-start | bytes 3145736 | tf_op jit(solution)/shard_map/ppermute | solution.py:27
  386.1 450.3 %collective-permute-start.10 = (f32[1,2048,512]{1,2,0:T(8,128)}, f32[1,2048,512]{1,2,0:T(8,128)}, u32[]{:S(2)}, u32[]{:S(2)}) collective-permute-start(f32[1,2048,512]{1,2,0:T(8,128)} %get-tuple-element.12), channel_id=1, source_target_pairs={{0,24},{8,0},{16,8},{24,16},{1,25},{9,1},{17,9},{25,17},{2,26},{10... | collective-permute-start | bytes 12582920 | tf_op jit(solution)/shard_map/ppermute | solution.py:27
  389.4 447.0 %collective-permute-start.9 = (f32[1,2048,512]{1,2,0:T(8,128)}, f32[1,2048,512]{1,2,0:T(8,128)}, u32[]{:S(2)}, u32[]{:S(2)}) collective-permute-start(f32[1,2048,512]{1,2,0:T(8,128)} %get-tuple-element.12), channel_id=1, source_target_pairs={{0,8},{8,16},{16,24},{24,0},{1,9},{9,17},{17,25},{25,1},{2,10},{10... | collective-permute-start | bytes 12582920 | tf_op jit(solution)/shard_map/ppermute | solution.py:27
  389.4 217.3 %collective-permute-start.8 = (f32[1,2048,128]{1,2,0:T(8,128)S(1)}, f32[1,2048,128]{1,2,0:T(8,128)S(1)}, u32[]{:S(2)}, u32[]{:S(2)}) collective-permute-start(f32[1,2048,128]{1,2,0:T(8,128)S(1)} %get-tuple-element.14), channel_id=1, source_target_pairs={{0,24},{8,0},{16,8},{24,16},{1,25},{9,1},{17,9},{25,17},{2,26},{10... | collective-permute-start | bytes 3145736 | tf_op jit(solution)/shard_map/ppermute | solution.py:27
  393.2 209.7 %collective-permute-start.2 = (f32[1]{0:T(128)}, f32[1]{0:T(128)}, u32[]{:S(2)}, u32[]{:S(2)}) collective-permute-start(f32[1]{0:T(128)} %param.15), channel_id=1, source_target_pairs={{0,8},{8,16},{16,24},{24,0},{1,9},{9,17},{17,25},{25,1},{2,10},{10... | collective-permute-start | bytes 20 | tf_op jit(solution)/shard_map/ppermute | solution.py:27
  602.9 248.1 %collective-permute-start.3 = (f32[1,2048,512]{1,2,0:T(8,128)}, f32[1,2048,512]{1,2,0:T(8,128)}, u32[]{:S(2)}, u32[]{:S(2)}) collective-permute-start(f32[1,2048,512]{1,2,0:T(8,128)} %get-tuple-element.13), channel_id=1, source_target_pairs={{0,8},{8,16},{16,24},{24,0},{1,9},{9,17},{17,25},{25,1},{2,10},{10... | collective-permute-start | bytes 12582920 | tf_op jit(solution)/shard_map/ppermute | solution.py:27
  602.9 248.1 %collective-permute-start.4 = (f32[1,2048,512]{1,2,0:T(8,128)}, f32[1,2048,512]{1,2,0:T(8,128)}, u32[]{:S(2)}, u32[]{:S(2)}) collective-permute-start(f32[1,2048,512]{1,2,0:T(8,128)} %get-tuple-element.13), channel_id=1, source_target_pairs={{0,24},{8,0},{16,8},{24,16},{1,25},{9,1},{17,9},{25,17},{2,26},{10... | collective-permute-start | bytes 12582920 | tf_op jit(solution)/shard_map/ppermute | solution.py:27
  606.7 202.5 %collective-permute-start.5 = (f32[1,2048,128]{1,2,0:T(8,128)S(1)}, f32[1,2048,128]{1,2,0:T(8,128)S(1)}, u32[]{:S(2)}, u32[]{:S(2)}) collective-permute-start(f32[1,2048,128]{1,2,0:T(8,128)S(1)} %get-tuple-element.15), channel_id=1, source_target_pairs={{0,8},{8,16},{16,24},{24,0},{1,9},{9,17},{17,25},{25,1},{2,10},{10... | collective-permute-start | bytes 3145736 | tf_op jit(solution)/shard_map/ppermute | solution.py:27
  810.2 22.5 %collective-permute-start.6 = (f32[1,2048,128]{1,2,0:T(8,128)S(1)}, f32[1,2048,128]{1,2,0:T(8,128)}, u32[]{:S(2)}, u32[]{:S(2)}) collective-permute-start(f32[1,2048,128]{1,2,0:T(8,128)S(1)} %get-tuple-element.15), channel_id=1, source_target_pairs={{0,24},{8,0},{16,8},{24,16},{1,25},{9,1},{17,9},{25,17},{2,26},{10... | collective-permute-start | bytes 3145736 | tf_op jit(solution)/shard_map/ppermute | solution.py:27
  (3 other events, 3.4 us)
Sparse Core Ops, SparseCore 0:
  9.6 47.9 all-gather.2
  59.1 129.9 all-gather.4
  243.5 121.8 reduce-scatter.1
